TPU v7x, 512 devices: a whole 4x4x16 slice. The times are simulated.
512 devices in a mesh: seq: 128 (over x, y, z_lo, core), head: 4 (over z_hi).
Axes of the slice: x: 4, y: 4, z: 16 (z_hi: 4, z_lo: 4; z = z_hi * 4 + z_lo), core: 2. Of those that a mesh axis runs over, the one named last changes fastest.
Arguments:
- queries: bfloat16 [16, 32768, 128], P('head', 'seq'), may hold values from -9 to 9
- key_vectors: bfloat16 [16, 32768, 128], P('head', 'seq'), may hold values from -9 to 9
- value_vectors: bfloat16 [16, 32768, 128], P('head', 'seq'), may hold values from -16 to 16
- block_perm: int32 [16, 64], P('head'), may hold values from 0 to 63, each once within a row
- out_weight: bfloat16 [16, 128, 2048], P('head'), may hold values from -0.125 to 0.125
- out_cotangent: bfloat16 [32768, 2048], P('seq', 'head'), may hold values from -6 to 6
Outputs:
- projected: bfloat16 [32768, 2048], P('seq', 'head')
- gradient_of_queries: bfloat16 [16, 32768, 128], P('head', 'seq')
- key_grad: bfloat16 [16, 32768, 128], P('head', 'seq')
- value_grad: bfloat16 [16, 32768, 128], P('head', 'seq')
Inputs may be any that keep to these rules, and one draw needn't show every extreme that they name: Each row of block_perm names every block of 0 to 63 once.
All inputs are finite; a program needn't handle non-finite values.
Results may differ from a plain program's by a relative error of at most 0.029.
Values may be sent and summed in bfloat16 or wider, within the bound.
A program may use at most 64 MiB of HBM per device.

v0:
```python
import math

import jax
import jax.numpy as jnp
from jax import lax
from jax.sharding import PartitionSpec as P


def partner(shard, axis, bit):
    return lax.ppermute(shard, axis, [(i, i ^ 1 << bit) for i in range(lax.axis_size(axis))])


def per_device(queries, key_vectors, value_vectors, block_perm, out_weight, out_cotangent):
    devices = lax.axis_size("seq")
    position = lax.axis_index("seq")
    parity = position % 2
    group_heads, tok_rows, head_width = queries.shape
    portion = tok_rows * head_width // devices
    score_scale = 1.0 / math.sqrt(head_width)
    owners = jnp.repeat(block_perm, 2, axis=1)
    indices = lax.iota(jnp.int32, devices)
    sources = [2 * owners, 2 * owners + 1]
    source_table = jnp.stack(sources, axis=1)
    slot_count = source_table.shape[1]
    select = (source_table[..., None] == indices).astype(jnp.bfloat16)
    stacked = jnp.stack([key_vectors, value_vectors])
    spread = lax.all_to_all(
        stacked.reshape(2, group_heads, devices, portion),
        "seq",
        split_axis=2,
        concat_axis=2,
        tiled=True,
    )
    picked = jnp.einsum(
        "hsij,chjl->chsil", select, spread, preferred_element_type=jnp.float32
    ).astype(jnp.bfloat16)
    routed = lax.all_to_all(picked, "seq", split_axis=3, concat_axis=3, tiled=True)
    routed = routed.reshape(2, group_heads, slot_count, tok_rows, head_width)
    partner_kv = routed.reshape(2, group_heads, 2 * tok_rows, head_width)
    pair_other = partner(stacked, "seq", 0)
    local_kv = jnp.where(
        parity == 0,
        jnp.concatenate([stacked, pair_other], 2),
        jnp.concatenate([pair_other, stacked], 2),
    )
    combined = jnp.concatenate([local_kv, partner_kv], 2)
    key_all = combined[0]
    value_all = combined[1]
    logit_scores = (
        jnp.einsum("htd,hkd->htk", queries, key_all, preferred_element_type=jnp.float32)
        * score_scale
    )
    row_max = jnp.max(logit_scores, axis=-1, keepdims=True)
    weights = jnp.exp(logit_scores - row_max)
    probabilities = weights / jnp.sum(weights, axis=-1, keepdims=True)
    reduced_probabilities = probabilities.astype(jnp.bfloat16)
    attention_result = jnp.einsum(
        "htk,hkd->htd", reduced_probabilities, value_all, preferred_element_type=jnp.float32
    ).astype(jnp.bfloat16)
    partial_out = jnp.einsum(
        "htd,hde->te", attention_result, out_weight, preferred_element_type=jnp.float32
    )
    summed = lax.psum(partial_out.astype(jnp.bfloat16), "head").astype(jnp.float32)
    columns = summed.shape[1] // lax.axis_size("head")
    result = lax.dynamic_slice_in_dim(summed, lax.axis_index("head") * columns, columns, 1)
    projected = result.astype(jnp.bfloat16)
    full_grad = lax.all_gather(out_cotangent, "head", axis=1, tiled=True)
    grad_att = jnp.einsum(
        "te,hde->htd", full_grad, out_weight, preferred_element_type=jnp.float32
    ).astype(jnp.bfloat16)
    row_delta = jnp.sum(
        grad_att.astype(jnp.float32) * attention_result.astype(jnp.float32), axis=-1, keepdims=True
    )
    probability_gradient = jnp.einsum(
        "htd,hkd->htk", grad_att, value_all, preferred_element_type=jnp.float32
    )
    score_gradient = (probabilities * (probability_gradient - row_delta) * score_scale).astype(
        jnp.bfloat16
    )
    gradient_of_queries = jnp.einsum(
        "htk,hkd->htd", score_gradient, key_all, preferred_element_type=jnp.float32
    ).astype(jnp.bfloat16)
    key_part = jnp.einsum(
        "htk,htd->hkd", score_gradient, queries, preferred_element_type=jnp.float32
    )
    value_part = jnp.einsum(
        "htk,htd->hkd", reduced_probabilities, grad_att, preferred_element_type=jnp.float32
    )
    gradients = jnp.stack([key_part, value_part])
    block_rows = 2 * tok_rows
    local_grad = gradients[:, :, :block_rows].reshape(2, group_heads, 2, tok_rows, head_width)
    own_grad = jnp.where(parity == 0, local_grad[:, :, 0], local_grad[:, :, 1])
    other_grad = jnp.where(parity == 0, local_grad[:, :, 1], local_grad[:, :, 0]).astype(
        jnp.bfloat16
    )
    partner_grad = gradients[:, :, block_rows:].reshape(2, group_heads, 2, tok_rows, head_width)
    partner_grad = partner_grad.astype(jnp.bfloat16)
    returned = lax.all_to_all(
        partner_grad.reshape(2, group_heads, slot_count, devices, portion),
        "seq",
        split_axis=3,
        concat_axis=3,
        tiled=True,
    )
    summed_back = jnp.einsum(
        "hsij,chsil->chjl", select, returned, preferred_element_type=jnp.float32
    ).astype(jnp.bfloat16)
    arrived = lax.all_to_all(summed_back, "seq", split_axis=2, concat_axis=2, tiled=True)
    arrived = arrived.reshape(2, group_heads, tok_rows, head_width).astype(jnp.float32)
    pair_back = partner(other_grad, "seq", 0).astype(jnp.float32)
    total_grad = own_grad + arrived + pair_back
    key_grad = total_grad[0].astype(jnp.bfloat16)
    value_grad = total_grad[1].astype(jnp.bfloat16)
    return (projected, gradient_of_queries, key_grad, value_grad)


def solution(mesh):
    return jax.shard_map(
        per_device,
        mesh=mesh,
        in_specs=(
            P("head", "seq", None),
            P("head", "seq", None),
            P("head", "seq", None),
            P("head", None),
            P("head", None, None),
            P("seq", "head"),
        ),
        out_specs=(
            P("seq", "head"),
            P("head", "seq", None),
            P("head", "seq", None),
            P("head", "seq", None),
        ),
        check_vma=False,
    )
```

profile of v0, /device:TPU:1, one launch (start us, length us, event | category | flops | bytes accessed | tf_op | source)
XLA Modules:
  0.0 314.6 jit_solution(3298835082028819904)
XLA Ops:
  7.2 1.2 stack.33
  8.4 1.0 stack.32
  9.5 1.3 copy.72
  10.8 13.8 %all-to-all-start = ((bf16[2,4,128,256]{3,0,1,2:T(2,128)(2,1)}), bf16[2,4,128,256]{3,0,1,2:T(2,128)(2,1)S(1)}, u32[]{:S(2)}, u32[]{:S(2)}) async-start(bf16[2,4,128,256]{3,0,1,2:T(2,128)(2,1)} %copy.72), calls=%async_computation | async-start | bytes 1048576 | tf_op jit(solution)/shard_map/all_to_all | solution.py:27
  24.9 18.0 %all-to-all-done = bf16[2,4,128,256]{3,0,1,2:T(2,128)(2,1)S(1)} async-done(((bf16[2,4,128,256]{3,0,1,2:T(2,128)(2,1)}), bf16[2,4,128,256]{3,0,1,2:T(2,128)(2,1)S(1)}, u32[]{:S(2)}, u32[]{:S(2)}) %all-to-all-start) | async-done | bytes 524320 | tf_op jit(solution)/shard_map/all_to_all | solution.py:27
  43.0 0.8 copy-done.14
  43.8 1.7 fusion.11
  45.5 2.1 copy.76
  47.5 7.5 %all-to-all-start.1 = ((bf16[2,4,2,128,256]{4,2,0,1,3:T(2,128)(2,1)}), bf16[2,4,2,128,256]{4,2,0,1,3:T(2,128)(2,1)}, u32[]{:S(2)}, u32[]{:S(2)}) async-start(bf16[2,4,2,128,256]{4,2,0,1,3:T(2,128)(2,1)} %copy.76), calls=%async_computation.1 | async-start | bytes 2097152 | tf_op jit(solution)/shard_map/all_to_all | solution.py:37
  55.2 3.2 %collective-permute-start = (bf16[2,4,256,128]{3,2,1,0:T(8,128)(2,1)S(1)}, bf16[2,4,256,128]{3,2,1,0:T(8,128)(2,1)}, u32[]{:S(2)}, u32[]{:S(2)}) collective-permute-start(bf16[2,4,256,128]{3,2,1,0:T(8,128)(2,1)S(1)} %pad_maximum_fusion.2), channel_id=1, source_target_pairs={{0,4},{4,0},{8,12},{12,8},{16,20},{20,16},{24,28},{28,24},{32,36},... | collective-permute-start | bytes 1572872 | tf_op jit(solution)/shard_map/ppermute | solution.py:10
  58.4 1.4 collective-permute-done
  59.9 1.6 maximum_select_fusion
  61.5 22.8 %all-to-all-done.1 = bf16[2,4,2,128,256]{4,2,0,1,3:T(2,128)(2,1)} async-done(((bf16[2,4,2,128,256]{4,2,0,1,3:T(2,128)(2,1)}), bf16[2,4,2,128,256]{4,2,0,1,3:T(2,128)(2,1)}, u32[]{:S(2)}, u32[]{:S(2)}) %all-to-all-start.1) | async-done | bytes 1048608 | tf_op jit(solution)/shard_map/all_to_all | solution.py:37
  84.4 2.5 copy.77
  86.9 2.3 reshape_reshape.3
  89.2 2.1 fusion.15
  91.3 4.6 %fusion.36 = (f32[4,256]{1,0:T(4,128)S(1)}, f32[4,256,1024]{1,2,0:T(8,128)}) fusion(bf16[4,1024,128]{2,1,0:T(8,128)(2,1)} %fusion.15, bf16[4,256,128]{2,1,0:T(8,128)(2,1)S(1)} %copy-done.15), kind=kOutput, calls=%fused_computation.63 | convolution fusion | flops 271582208 | bytes 5509120 | tf_op jit(solution)/shard_map/sub | solution.py:54
  95.9 2.6 fusion.10
  98.5 1.3 copy-done.3
  99.9 0.6 convolution_convert_fusion.3
  100.4 16.5 %all-gather.2.cloned.1.call-done = bf16[256,2048]{1,0:T(8,128)(2,1)} async-done(((bf16[256,512]{1,0:T(8,128)(2,1)}), bf16[256,2048]{1,0:T(8,128)(2,1)}) %all-gather.2.cloned.1.call-update) | async-done | bytes 1048592 | tf_op jit(solution)/shard_map/all_gather | solution.py:67
  116.9 2.1 fusion.22
  119.1 0.7 convolution_bitcast_fusion.1
  119.8 0.3 copy-done.11
  120.1 0.5 copy-done.7
  120.6 0.8 multiply_convert_fusion
  121.5 0.7 convolution_bitcast_fusion.2
  122.2 0.6 copy-done.8
  122.8 1.3 copy-done.2
  124.1 0.2 fusion.8
  124.3 1.3 convert_element_type.88
  125.5 2.3 copy.86
  127.8 44.9 %all_to_all.20 = bf16[2,4,2,128,256]{4,2,0,1,3:T(2,128)(2,1)S(1)} all-to-all(bf16[2,4,2,128,256]{4,2,0,1,3:T(2,128)(2,1)S(1)} %copy.86), channel_id=1, replica_groups=mesh['seq'=128,'head'=4] {'seq'}, dimensions={3} | all-to-all | bytes 2097152 | tf_op jit(solution)/shard_map/all_to_all | solution.py:98
  172.7 0.9 fusion.13
  173.6 1.1 copy.88
  174.7 6.6 %all-to-all-start.3 = ((bf16[2,4,128,256]{3,0,1,2:T(2,128)(2,1)}), bf16[2,4,128,256]{3,0,1,2:T(2,128)(2,1)S(1)}, u32[]{:S(2)}, u32[]{:S(2)}) async-start(bf16[2,4,128,256]{3,0,1,2:T(2,128)(2,1)} %copy.88), calls=%async_computation.3 | async-start | bytes 1048576 | tf_op jit(solution)/shard_map/all_to_all | solution.py:108
  181.3 1.8 fusion.6
  183.2 1.8 fusion.7
  185.0 1.3 copy-done.5
  186.3 0.9 fusion.21
  187.2 2.9 collective-permute-start.1
  190.1 1.6 convolution_convert_fusion.1
  191.7 109.2 %all-reduce.2.cloned.1.call-done = bf16[256,2048]{1,0:T(8,128)(2,1)} async-done(((bf16[256,2048]{1,0:T(8,128)(2,1)}), bf16[256,2048]{1,0:T(8,128)(2,1)}) %all-reduce.2.cloned.1.call-update) | async-done | bytes 1048592 | tf_op jit(solution)/shard_map/psum | solution.py:63
  300.9 1.7 convert_convert_fusion
  302.6 1.1 copy_convert_fusion
  303.7 1.3 reshape.55
  305.0 1.9 fusion.18
  306.9 0.8 slice_bitcast_fusion.2
  (43 shorter events, 0.6 us)
Async XLA Ops:
  7.2 109.8 %copy-start = (bf16[4,128,2048]{2,1,0:T(8,128)(2,1)S(1)}, bf16[4,128,2048]{2,1,0:T(8,128)(2,1)}, u32[]{:S(2)}) copy-start(bf16[4,128,2048]{2,1,0:T(8,128)(2,1)} %param.10) | copy-start | bytes 6291460
  7.2 17.5 %copy-start.17 = (s32[4,64]{1,0:T(4,128)S(1)}, s32[4,64]{1,0:T(4,128)}, u32[]{:S(2)}) copy-start(s32[4,64]{1,0:T(4,128)} %param.9) | copy-start | bytes 3076
  10.8 32.1 %all-to-all-start = ((bf16[2,4,128,256]{3,0,1,2:T(2,128)(2,1)}), bf16[2,4,128,256]{3,0,1,2:T(2,128)(2,1)S(1)}, u32[]{:S(2)}, u32[]{:S(2)}) async-start(bf16[2,4,128,256]{3,0,1,2:T(2,128)(2,1)} %copy.72), calls=%async_computation | async-start | bytes 1048576 | tf_op jit(solution)/shard_map/all_to_all | solution.py:27
  43.0 0.8 copy-start.14
  45.4 9.7 %copy-start.12 = (bf16[4,256,128]{2,1,0:T(8,128)(2,1)S(1)}, bf16[4,256,128]{2,1,0:T(8,128)(2,1)}, u32[]{:S(2)}) copy-start(bf16[4,256,128]{2,1,0:T(8,128)(2,1)} %param.8) | copy-start | bytes 786436
  47.5 7.6 %copy-start.13 = (bf16[4,256,128]{2,1,0:T(8,128)(2,1)S(1)}, bf16[4,256,128]{2,1,0:T(8,128)(2,1)}, u32[]{:S(2)}) copy-start(bf16[4,256,128]{2,1,0:T(8,128)(2,1)} %param.7) | copy-start | bytes 786436
  47.5 36.8 %all-to-all-start.1 = ((bf16[2,4,2,128,256]{4,2,0,1,3:T(2,128)(2,1)}), bf16[2,4,2,128,256]{4,2,0,1,3:T(2,128)(2,1)}, u32[]{:S(2)}, u32[]{:S(2)}) async-start(bf16[2,4,2,128,256]{4,2,0,1,3:T(2,128)(2,1)} %copy.76), calls=%async_computation.1 | async-start | bytes 2097152 | tf_op jit(solution)/shard_map/all_to_all | solution.py:37
  55.1 61.8 %all-gather.2.cloned.1.call-start = ((), (), s32[]{:S(2)}) async-start(), calls=%async_computation.5 | async-start | bytes 1310720 | tf_op jit(solution)/shard_map/all_gather | solution.py:67
  55.2 4.6 %collective-permute-start = (bf16[2,4,256,128]{3,2,1,0:T(8,128)(2,1)S(1)}, bf16[2,4,256,128]{3,2,1,0:T(8,128)(2,1)}, u32[]{:S(2)}, u32[]{:S(2)}) collective-permute-start(bf16[2,4,256,128]{3,2,1,0:T(8,128)(2,1)S(1)} %pad_maximum_fusion.2), channel_id=1, source_target_pairs={{0,4},{4,0},{8,12},{12,8},{16,20},{20,16},{24,28},{28,24},{32,36},... | collective-permute-start | bytes 1572872 | tf_op jit(solution)/shard_map/ppermute | solution.py:10
  89.2 2.1 copy-start.15
  95.9 4.0 %copy-start.6 = (bf16[2,4,512,128]{3,2,1,0:T(8,128)(2,1)S(1)}, bf16[2,4,512,128]{3,2,1,0:T(8,128)(2,1)}, u32[]{:S(2)}) copy-start(bf16[2,4,512,128]{3,2,1,0:T(8,128)(2,1)} %reshape_reshape.3) | copy-start | bytes 3145732
  98.5 1.3 copy-start.3
  116.9 2.1 copy-start.4
  116.9 3.1 copy-start.11
  119.1 1.5 copy-start.7
  119.8 2.4 copy-start.1
  120.5 0.9 copy-start.16
  121.5 1.3 copy-start.8
  122.8 1.3 copy-start.2
  174.7 127.9 %all-to-all-start.3 = ((bf16[2,4,128,256]{3,0,1,2:T(2,128)(2,1)}), bf16[2,4,128,256]{3,0,1,2:T(2,128)(2,1)S(1)}, u32[]{:S(2)}, u32[]{:S(2)}) async-start(bf16[2,4,128,256]{3,0,1,2:T(2,128)(2,1)} %copy.88), calls=%async_computation.3 | async-start | bytes 1048576 | tf_op jit(solution)/shard_map/all_to_all | solution.py:108
  181.3 119.7 %all-reduce.2.cloned.1.call-start = ((), (), s32[]{:S(2)}) async-start(), calls=%async_computation.4 | async-start | bytes 2097152 | tf_op jit(solution)/shard_map/psum | solution.py:63
  183.1 6.9 %copy-start.9 = (bf16[4,256,1024]{1,2,0:T(8,128)(2,1)S(1)}, bf16[4,256,1024]{1,2,0:T(8,128)(2,1)}, u32[]{:S(2)}) copy-start(bf16[4,256,1024]{1,2,0:T(8,128)(2,1)} %copy-done.8) | copy-start | bytes 6291460
  183.1 6.9 %copy-start.10 = (bf16[4,1024,128]{2,1,0:T(8,128)(2,1)S(1)}, bf16[4,1024,128]{2,1,0:T(8,128)(2,1)}, u32[]{:S(2)}) copy-start(bf16[4,1024,128]{2,1,0:T(8,128)(2,1)} %fusion.15) | copy-start | bytes 3145732
  185.0 1.3 copy-start.5
  187.2 117.8 %collective-permute-start.1 = (bf16[2,4,256,128]{3,2,1,0:T(8,128)(2,1)}, bf16[2,4,256,128]{3,2,1,0:T(8,128)(2,1)}, u32[]{:S(2)}, u32[]{:S(2)}) collective-permute-start(bf16[2,4,256,128]{3,2,1,0:T(8,128)(2,1)} %fusion.21), channel_id=1, source_target_pairs={{0,4},{4,0},{8,12},{12,8},{16,20},{20,16},{24,28},{28,24},{32,36},... | collective-permute-start | bytes 1572872 | tf_op jit(solution)/shard_map/ppermute | solution.py:10
Sparse Core Ops, SparseCore 0:
  58.5 58.3 all-gather.1
  185.1 115.8 all-reduce.1
where the time goes:
time: 316 us; the launch traced here: 315 us
  waiting for transfers between devices  168 us (53%)
  blocking collectives  44.9 us (14%)
  starting transfers between devices  34.1 us (11%)
  local copies, waits for them, and re-layouts  23.7 us (8%)
  matrix products  15.4 us (5%)
  between operations  14.4 us (5%)
  other arithmetic  14.1 us (4%)
    psum x1, waiting for transfers between devices, per_device(): lax.psum(partial_out.astype(jnp.bfloat16), 'head').astype(jnp.float32)  109 us
    all_to_all x1, blocking collectives, per_device(): lax.all_to_all(partner_grad.reshape(2, group_heads, slot_count, devices,...  44.9 us
    all_to_all x1, waiting for transfers between devices, per_device(): lax.all_to_all(picked, 'seq', split_axis=3, concat_axis=3, tiled=True)  22.8 us
    all_to_all x1, waiting for transfers between devices, per_device(): lax.all_to_all(stacked.reshape(2, group_heads, devices, portion), 'seq',...  18 us
    all_gather x1, waiting for transfers between devices, per_device(): full_grad = lax.all_gather(out_cotangent, 'head', axis=1, tiled=True)  16.5 us
    all_to_all x1, starting transfers between devices, per_device(): lax.all_to_all(stacked.reshape(2, group_heads, devices, portion), 'seq',...  13.8 us
    all_to_all x1, starting transfers between devices, per_device(): lax.all_to_all(picked, 'seq', split_axis=3, concat_axis=3, tiled=True)  7.54 us
    all_to_all x1, starting transfers between devices, per_device(): lax.all_to_all(summed_back, 'seq', split_axis=2, concat_axis=2, tiled=True)  6.57 us
  transfers between devices with their start and end apart: 7, of which 5 were waited for; matrix products, arithmetic and copies ran while one was open for 9% of the time, Pallas kernels for 0%

commit v1 on v0

v1 whole, which is shorter than its diff:
```python
import functools
import math

import jax
import jax.numpy as jnp
from jax import lax
from jax.experimental import pallas as pl
from jax.experimental.pallas import tpu as pltpu
from jax.sharding import PartitionSpec as P

MESH = pl.DeviceIdType.MESH
BF = jnp.bfloat16
F32 = jnp.float32


def nn(a, b):
    return lax.dot_general(a, b, (((1,), (0,)), ((), ())), preferred_element_type=F32)


def nt(a, b):
    return lax.dot_general(a, b, (((1,), (1,)), ((), ())), preferred_element_type=F32)


def tn(a, b):
    return lax.dot_general(a, b, (((0,), (0,)), ((), ())), preferred_element_type=F32)


def peer_chip(me, step, chips):
    if chips != 64:
        return lax.rem(me + step, chips)
    out = 0
    for unit in (16, 4, 1):
        digit = lax.rem(lax.div(me, unit), 4) + lax.rem(lax.div(step, unit), 4)
        out = out + unit * lax.rem(digit, 4)
    return out


def kernel(
    dims,
    perm_ref, inv_ref, q_hbm, k_hbm, v_hbm, w_hbm, cot_hbm,
    proj_ref, dq_ref, dk_ref, dv_ref,
    kv, q, w, cot, in1, out1, in3, out3, back, prob, att, grad, att_t, grad_t,
    own, give, got, part, rs_far, rs_near,
    load_sem, a2a_send, a2a_recv, pair_send, pair_recv, ag_send, ag_recv, rs_send, rs_recv,
):
    heads, tok, width, chips, groups = dims
    seq = lax.axis_index("seq")
    hi = lax.axis_index("head")
    core = lax.rem(seq, 2)
    me = lax.div(seq, 2)
    sibling = {"seq": me * 2 + 1 - core}
    up, down = lax.rem(hi + 1, groups), lax.rem(hi + groups - 1, groups)
    far = lax.rem(hi + 2, groups)
    to_up, to_down = {"head": up}, {"head": down}
    per_head = chips // (2 * heads)
    mid = tok // 2
    my_head = lax.rem(lax.div(me, per_head), heads)
    scale = 1.0 / math.sqrt(width)

    def on_chip(p):
        return {"seq": p * 2 + core}

    def remote(src, dst, send, recv, where):
        return pltpu.make_async_remote_copy(
            src_ref=src, dst_ref=dst, send_sem=send, recv_sem=recv,
            device_id=where, device_id_type=MESH,
        )

    def arrived(ref, sem):
        pltpu.make_async_copy(ref, ref, sem).wait()

    half = chips // 2
    load_k = pltpu.make_async_copy(k_hbm, kv.at[0, pl.ds(0, half)], load_sem.at[0])
    load_v = pltpu.make_async_copy(v_hbm, kv.at[0, pl.ds(half, half)], load_sem.at[1])
    load_cot = pltpu.make_async_copy(cot_hbm, cot.at[hi], load_sem.at[2])
    load_q = pltpu.make_async_copy(q_hbm, q, load_sem.at[3])
    cols = cot_hbm.shape[1]
    load_w = [
        pltpu.make_async_copy(w_hbm.at[:, pl.ds(c * cols, cols)], w.at[c], load_sem.at[4 + c])
        for c in range(groups)
    ]
    for copy in [load_k, load_v, load_cot, load_q] + load_w:
        copy.start()

    barrier = pltpu.get_barrier_semaphore()

    def greet(step, carry):
        pl.semaphore_signal(
            barrier, inc=1, device_id=on_chip(peer_chip(me, step, chips)), device_id_type=MESH
        )
        return carry

    lax.fori_loop(1, chips, greet, 0)
    for where in (sibling, to_up, to_down):
        pl.semaphore_signal(barrier, inc=1, device_id=where, device_id_type=MESH)
    load_k.wait()
    load_v.wait()
    pl.semaphore_wait(barrier, chips - 1 + 3)

    def spread(src, dst, phase):
        def body(step, carry):
            p = peer_chip(me, step, chips)
            remote(src.at[p], dst.at[me], a2a_send.at[phase], a2a_recv.at[phase], on_chip(p)).start()
            return carry

        lax.fori_loop(1, chips, body, 0)
        dst[me] = src[me]

    def forward(src, table, out, dst, phase):
        def body(step, carry):
            p = peer_chip(me, step, chips)
            out[p] = src[table[my_head, p]]
            remote(out.at[p], dst.at[me], a2a_send.at[phase], a2a_recv.at[phase], on_chip(p)).start()
            return carry

        lax.fori_loop(1, chips, body, 0)
        dst[me] = src[table[my_head, me]]

    def all_arrived(dst, phase):
        arrived(dst.at[pl.ds(0, chips - 1)], a2a_recv.at[phase])

    spread(kv.at[0], in1, 0)
    swap_own = remote(kv.at[0], kv.at[1], pair_send.at[0], pair_recv.at[0], sibling)
    swap_own.start()

    load_cot.wait()
    lo, top = pl.ds(0, mid), pl.ds(mid, mid)
    ag_up = [
        remote(cot.at[hi, s], cot.at[hi, s], ag_send.at[i], ag_recv.at[i], to_up)
        for i, s in enumerate((lo, top))
    ]
    ag_down = [
        remote(cot.at[hi, s], cot.at[hi, s], ag_send.at[2 + i], ag_recv.at[2 + i], to_down)
        for i, s in enumerate((top, lo))
    ]
    for copy in (ag_up[0], ag_down[0], ag_up[1], ag_down[1]):
        copy.start()

    all_arrived(in1, 0)
    forward(in1, perm_ref, out1, kv.at[2], 1)

    ag_up[0].wait_recv()
    pass_up = remote(cot.at[down, lo], cot.at[down, lo], ag_send.at[4], ag_recv.at[4], to_up)
    pass_up.start()
    ag_down[0].wait_recv()
    pass_down = remote(cot.at[up, top], cot.at[up, top], ag_send.at[5], ag_recv.at[5], to_down)
    pass_down.start()

    load_q.wait()
    all_arrived(kv.at[2], 1)
    swap_partner = remote(kv.at[2], kv.at[3], pair_send.at[1], pair_recv.at[1], sibling)
    swap_partner.start()
    swap_own.wait_recv()
    swap_partner.wait_recv()

    def rows_of(slot, which, h):
        piece = kv[slot, pl.ds((which * heads + h) * per_head, per_head)]
        return piece.reshape(tok, width)

    def attend(h, carry):
        q_h = q[h]
        scores = [nt(rows_of(slot, 0, h), q_h) for slot in range(4)]
        top_score = functools.reduce(
            jnp.maximum, [jnp.max(s, axis=0, keepdims=True) for s in scores]
        )
        weights = [jnp.exp2((s - top_score) * (scale * math.log2(math.e))) for s in scores]
        total = functools.reduce(
            jnp.add, [jnp.sum(e, axis=0, keepdims=True) for e in weights]
        )
        inverse = 1.0 / total
        acc = None
        for slot in range(4):
            low = (weights[slot] * inverse).astype(BF)
            prob[h, slot] = low
            term = tn(rows_of(slot, 1, h), low)
            acc = term if acc is None else acc + term
        low = acc.astype(BF)
        att_t[h] = low
        att[h] = low.T
        return carry

    lax.fori_loop(0, heads, attend, 0)

    for copy in load_w:
        copy.wait()

    def project(c):
        acc = None
        for h in range(heads):
            term = nn(att[h], w[c, pl.ds(h * width, width)])
            acc = term if acc is None else acc + term
        part[c] = acc.astype(BF)

    project(far)
    rs_a = remote(part.at[far, lo], rs_far.at[0], rs_send.at[0], rs_recv.at[0], to_up)
    rs_b = remote(part.at[far, top], rs_far.at[1], rs_send.at[1], rs_recv.at[1], to_down)
    rs_a.start()
    rs_b.start()
    project(up)
    rs_c = remote(part.at[up, top], rs_near.at[0, top], rs_send.at[2], rs_recv.at[2], to_up)
    rs_c.start()
    project(down)
    rs_d = remote(part.at[down, lo], rs_near.at[1, lo], rs_send.at[3], rs_recv.at[3], to_down)
    rs_d.start()
    project(hi)

    ag_up[1].wait_recv()
    ag_down[1].wait_recv()
    pass_up.wait_recv()
    pass_down.wait_recv()

    def pull(h, carry):
        acc = None
        for c in range(groups):
            term = nt(cot[c], w[c, pl.ds(pl.multiple_of(h * width, width), width)])
            acc = term if acc is None else acc + term
        low = acc.astype(BF)
        grad[h] = low
        grad_t[h] = low.T
        return carry

    lax.fori_loop(0, heads, pull, 0)

    def differentiate(h, carry):
        q_h = q[h]
        grad_h = grad[h]
        delta = jnp.sum(
            grad_t[h].astype(F32) * att_t[h].astype(F32), axis=0, keepdims=True
        )
        dq_t = None
        for slot in range(4):
            low = prob[h, slot]
            d_prob = nt(rows_of(slot, 1, h), grad_h)
            d_score = (low.astype(F32) * ((d_prob - delta) * scale)).astype(BF)
            term = tn(rows_of(slot, 0, h), d_score)
            dq_t = term if dq_t is None else dq_t + term
            d_key = nn(d_score, q_h)
            d_value = nn(low, grad_h)
            for which, value in ((0, d_key), (1, d_value)):
                value = value.reshape(per_head, tok // per_head, width)
                where = pl.ds((which * heads + h) * per_head, per_head)
                if slot == 0:
                    own[where] = value
                else:
                    give[slot - 1, where] = value.astype(BF)
        dq_ref[h] = dq_t.T.astype(BF)
        return carry

    lax.fori_loop(0, heads, differentiate, 0)

    swap_pair = remote(give.at[0], got.at[0], pair_send.at[2], pair_recv.at[2], sibling)
    swap_term = remote(give.at[2], got.at[1], pair_send.at[3], pair_recv.at[3], sibling)
    swap_term.start()
    swap_pair.start()
    swap_term.wait_recv()
    both = give[1].astype(F32) + got[1].astype(F32)
    give[1] = both.astype(BF)

    spread(give.at[1], in3, 2)

    rs_a.wait_recv()
    part[up, lo] = (part[up, lo].astype(F32) + rs_far[0].astype(F32)).astype(BF)
    rs_e = remote(part.at[up, lo], rs_near.at[0, lo], rs_send.at[4], rs_recv.at[4], to_up)
    rs_e.start()
    rs_b.wait_recv()
    part[down, top] = (part[down, top].astype(F32) + rs_far[1].astype(F32)).astype(BF)
    rs_f = remote(part.at[down, top], rs_near.at[1, top], rs_send.at[5], rs_recv.at[5], to_down)
    rs_f.start()

    all_arrived(in3, 2)
    forward(in3, inv_ref, out3, back, 3)

    swap_pair.wait_recv()
    for copy in (rs_c, rs_d, rs_e, rs_f):
        copy.wait_recv()
    proj_ref[...] = (
        part[hi].astype(F32) + rs_near[0].astype(F32) + rs_near[1].astype(F32)
    ).astype(BF)

    all_arrived(back, 3)

    def finish(h, carry):
        for which, ref in ((0, dk_ref), (1, dv_ref)):
            where = pl.ds((which * heads + h) * per_head, per_head)
            remote_sum = (back[where].astype(F32) + got[0, where].astype(F32)).astype(BF)
            total = own[where] + remote_sum.astype(F32)
            ref[h] = total.astype(BF).reshape(tok, width)
        return carry

    lax.fori_loop(0, heads, finish, 0)

    for phase, ref in enumerate((kv.at[0], out1, give.at[1], out3)):
        arrived(ref.at[pl.ds(0, chips - 1)], a2a_send.at[phase])
    for copy in (
        [swap_own, swap_partner, swap_pair, swap_term, pass_up, pass_down]
        + ag_up + ag_down + [rs_a, rs_b, rs_c, rs_d, rs_e, rs_f]
    ):
        copy.wait_send()


def per_device(queries, key_vectors, value_vectors, block_perm, out_weight, out_cotangent):
    chips = lax.axis_size("seq") // 2
    groups = lax.axis_size("head")
    heads, tok, width = queries.shape
    rows = 2 * heads * tok // chips
    cols = out_cotangent.shape[1]
    blocks = lax.iota(jnp.int32, chips)
    inverse = jnp.sum(
        jnp.where(block_perm[:, None, :] == blocks[None, :, None], blocks[None, None, :], 0), axis=2
    )
    any_space = pl.BlockSpec(memory_space=pl.ANY)
    smem = pl.BlockSpec(memory_space=pltpu.SMEM)
    vmem = pl.BlockSpec(memory_space=pltpu.VMEM)
    mat = jax.ShapeDtypeStruct((heads, tok, width), BF)
    pieces = (chips, rows, width)
    dma = pltpu.SemaphoreType.DMA
    scratch = [
        pltpu.VMEM((4,) + pieces, BF),
        pltpu.VMEM((heads, tok, width), BF),
        pltpu.VMEM((groups, heads * width, cols), BF),
        pltpu.VMEM((groups, tok, cols), BF),
        pltpu.VMEM(pieces, BF),
        pltpu.VMEM(pieces, BF),
        pltpu.VMEM(pieces, BF),
        pltpu.VMEM(pieces, BF),
        pltpu.VMEM(pieces, BF),
        pltpu.VMEM((heads, 4, tok, tok), BF),
        pltpu.VMEM((heads, tok, width), BF),
        pltpu.VMEM((heads, tok, width), BF),
        pltpu.VMEM((heads, width, tok), BF),
        pltpu.VMEM((heads, width, tok), BF),
        pltpu.VMEM(pieces, F32),
        pltpu.VMEM((3,) + pieces, BF),
        pltpu.VMEM((2,) + pieces, BF),
        pltpu.VMEM((groups, tok, cols), BF),
        pltpu.VMEM((2, tok // 2, cols), BF),
        pltpu.VMEM((2, tok, cols), BF),
        dma((8,)), dma((4,)), dma((4,)), dma((4,)), dma((4,)), dma((6,)), dma((6,)), dma((6,)), dma((6,)),
    ]
    return pl.pallas_call(
        functools.partial(kernel, (heads, tok, width, chips, groups)),
        out_shape=(jax.ShapeDtypeStruct((tok, cols), BF), mat, mat, mat),
        in_specs=[smem, smem] + [any_space] * 5,
        out_specs=(vmem,) * 4,
        scratch_shapes=scratch,
        compiler_params=pltpu.CompilerParams(
            collective_id=0, has_side_effects=True, vmem_limit_bytes=48 << 20
        ),
    )(
        block_perm,
        inverse,
        queries,
        key_vectors.reshape(chips // 2, rows, width),
        value_vectors.reshape(chips // 2, rows, width),
        out_weight.reshape(heads * width, -1),
        out_cotangent,
    )


def solution(mesh):
    return jax.shard_map(
        per_device,
        mesh=mesh,
        in_specs=(
            P("head", "seq", None),
            P("head", "seq", None),
            P("head", "seq", None),
            P("head", None),
            P("head", None, None),
            P("seq", "head"),
        ),
        out_specs=(
            P("seq", "head"),
            P("head", "seq", None),
            P("head", "seq", None),
            P("head", "seq", None),
        ),
        check_vma=False,
    )
```

time: 316 us -> 151 us (0.48)
  waiting for transfers between devices: 168 us -> 0 us
  Pallas kernels: 0 us -> 140 us
  blocking collectives: 44.9 us -> 0 us
  starting transfers between devices: 34.1 us -> 0 us
  matrix products: 15.4 us -> 0 us
  local copies, waits for them, and re-layouts: 23.7 us -> 8.88 us
  between operations: 14.4 us -> 0.65 us
  other arithmetic: 14.1 us -> 0.82 us
    pallas_call x0 -> x1, Pallas kernels: none -> 140 us  [per_device(): pl.pallas_call(functools.partial(kernel, (heads, tok, width, chips, group...]
    psum x1 -> x0, waiting for transfers between devices: 109 us -> none  [per_device(): lax.psum(partial_out.astype(jnp.bfloat16), 'head').astype(jnp.float32)]
    all_to_all x1 -> x0, blocking collectives: 44.9 us -> none  [per_device(): lax.all_to_all(partner_grad.reshape(2, group_heads, slot_count, devices,...]
    all_to_all x3 -> x0, waiting for transfers between devices: 40.9 us -> none  [the longest x1 22.8 us: per_device(): lax.all_to_all(picked, 'seq', split_axis=3, concat_axis=3, tiled=True)]
    all_to_all x3 -> x0, starting transfers between devices: 27.9 us -> none  [the longest x1 13.8 us: per_device(): lax.all_to_all(stacked.reshape(2, group_heads, devices, portion), 'seq',...]
    all_gather x1 -> x0, waiting for transfers between devices: 16.5 us -> none  [per_device(): full_grad = lax.all_gather(out_cotangent, 'head', axis=1, tiled=True)]
    dot_general x9 -> x0, matrix products: 10.8 us -> none  [the longest x1 2.13 us: per_device(): jnp.einsum('te,hde->htd', full_grad, out_weight, preferred_element_type=j...]
    convert_element_type x6 -> x0, local copies, waits for them, and re-layouts: 8.89 us -> none  [the longest x2 3.55 us: per_device(): partner_grad = partner_grad.astype(jnp.bfloat16)]
  transfers between devices with their start and end apart: 7 -> 0, of which waited for: 5 -> 0; matrix products, arithmetic and copies ran while one was open for 9% -> 0% of each run, Pallas kernels for 0% -> 0%
where the time goes in v1:
time: 151 us
  Pallas kernels  140 us (93%)
  local copies, waits for them, and re-layouts  8.88 us (6%)
    pallas_call x1, Pallas kernels, per_device(): pl.pallas_call(functools.partial(kernel, (heads, tok, width, chips, group...  140 us
    unnamed x16, local copies, waits for them, and re-layouts  8.88 us

profile of v1, /device:TPU:1, one launch (start us, length us, event | category | flops | bytes accessed | tf_op | source)
XLA Modules:
  0.0 150.8 jit_solution(8985184478164112617)
XLA Ops:
  0.6 0.8 select_reduce_fusion.inv_ref
  1.5 0.0 copy-start
  1.5 1.6 %copy-done = bf16[4,128,2048]{2,1,0:T(8,128)(2,1)S(1)} copy-done((bf16[4,128,2048]{2,1,0:T(8,128)(2,1)S(1)}, bf16[4,128,2048]{2,1,0:T(8,128)(2,1)}, u32[]{:S(2)}) %copy-start) | copy-done | bytes 2097176
  3.1 0.0 copy-start.1
  3.1 0.9 copy-done.1
  4.0 0.0 copy-start.2
  4.0 0.9 copy-done.2
  5.0 0.0 copy-start.3
  5.0 0.9 copy-done.3
  5.9 0.0 copy-start.4
  5.9 0.9 copy-done.4
  6.9 0.0 copy-start.5
  6.9 0.7 copy-done.5
  7.5 140.4 %shard_map.93 = (bf16[256,512]{1,0:T(8,128)(2,1)S(1)}, bf16[4,256,128]{2,1,0:T(8,128)(2,1)S(1)}, bf16[4,256,128]{2,1,0:T(8,128)(2,1)S(1)}, bf16[4,256,128]{2,1,0:T(8,128)(2,1)S(1)}) custom-call(s32[4,64]{1,0:T(4,128)S(1)} %copy-done.5, s32[4,64]{1,0:T(4,128)S(1)} %select_reduce_fusion.inv_ref, bf16[4,256,128]{2,1,0:T(8,128)(2,1)S(1)} %copy-done.1, ...), custom_call_target="tpu_custom_call" | custom-call | tf_op jit(solution)/shard_map/pallas_call | solution.py:340
  148.0 0.7 copy.14
  148.7 0.7 copy.15
  149.4 0.7 copy.16
  150.1 0.7 copy.17
Async XLA Ops:
  1.5 1.6 %copy-start = (bf16[4,128,2048]{2,1,0:T(8,128)(2,1)S(1)}, bf16[4,128,2048]{2,1,0:T(8,128)(2,1)}, u32[]{:S(2)}) copy-start(bf16[4,128,2048]{2,1,0:T(8,128)(2,1)} %param.10) | copy-start | bytes 6291460
  3.1 0.9 copy-start.1
  4.0 0.9 copy-start.2
  5.0 0.9 copy-start.3
  5.9 0.9 copy-start.4
  6.9 0.7 copy-start.5

commit v2 on v1

--- a/solution.py
+++ b/solution.py
@@ -25,13 +25,17 @@
     return lax.dot_general(a, b, (((0,), (0,)), ((), ())), preferred_element_type=F32)
 
 
+def digits(chips):
+    side = round(chips ** (1 / 3))
+    return (side * side, side, 1), side
+
+
 def peer_chip(me, step, chips):
-    if chips != 64:
-        return lax.rem(me + step, chips)
+    units, side = digits(chips)
     out = 0
-    for unit in (16, 4, 1):
-        digit = lax.rem(lax.div(me, unit), 4) + lax.rem(lax.div(step, unit), 4)
-        out = out + unit * lax.rem(digit, 4)
+    for unit in units:
+        digit = lax.rem(lax.div(me, unit), side) + lax.rem(lax.div(step, unit), side)
+        out = out + unit * lax.rem(digit, side)
     return out
 
 
@@ -39,9 +43,10 @@
     dims,
     perm_ref, inv_ref, q_hbm, k_hbm, v_hbm, w_hbm, cot_hbm,
     proj_ref, dq_ref, dk_ref, dv_ref,
-    kv, q, w, cot, in1, out1, in3, out3, back, prob, att, grad, att_t, grad_t,
-    own, give, got, part, rs_far, rs_near,
-    load_sem, a2a_send, a2a_recv, pair_send, pair_recv, ag_send, ag_recv, rs_send, rs_recv,
+    kv, q, w, wx, cot, cot_m, gp_out, gp_in, g_acc,
+    in1, out1, in3, out3, back, prob, att, att_m, att_t, grad, pp_out, pp_in,
+    own, give, got,
+    load_sem, a2a_send, a2a_recv, pair_send, pair_recv, wx_send, wx_recv, hd_send, hd_recv,
 ):
     heads, tok, width, chips, groups = dims
     seq = lax.axis_index("seq")
@@ -49,11 +54,10 @@
     core = lax.rem(seq, 2)
     me = lax.div(seq, 2)
     sibling = {"seq": me * 2 + 1 - core}
-    up, down = lax.rem(hi + 1, groups), lax.rem(hi + groups - 1, groups)
-    far = lax.rem(hi + 2, groups)
-    to_up, to_down = {"head": up}, {"head": down}
+    near = (hi + 1 - 2 * lax.rem(hi, 2), groups - 1 - hi)
     per_head = chips // (2 * heads)
     mid = tok // 2
+    side_rows = (pl.ds(0, mid), pl.ds(mid, mid))
     my_head = lax.rem(lax.div(me, per_head), heads)
     scale = 1.0 / math.sqrt(width)
 
@@ -72,14 +76,14 @@
     half = chips // 2
     load_k = pltpu.make_async_copy(k_hbm, kv.at[0, pl.ds(0, half)], load_sem.at[0])
     load_v = pltpu.make_async_copy(v_hbm, kv.at[0, pl.ds(half, half)], load_sem.at[1])
-    load_cot = pltpu.make_async_copy(cot_hbm, cot.at[hi], load_sem.at[2])
+    load_cot = pltpu.make_async_copy(cot_hbm, cot, load_sem.at[2])
     load_q = pltpu.make_async_copy(q_hbm, q, load_sem.at[3])
     cols = cot_hbm.shape[1]
     load_w = [
         pltpu.make_async_copy(w_hbm.at[:, pl.ds(c * cols, cols)], w.at[c], load_sem.at[4 + c])
         for c in range(groups)
     ]
-    for copy in [load_k, load_v, load_cot, load_q] + load_w:
+    for copy in [load_k, load_v] + load_w + [load_cot, load_q]:
         copy.start()
 
     barrier = pltpu.get_barrier_semaphore()
@@ -91,11 +95,35 @@
         return carry
 
     lax.fori_loop(1, chips, greet, 0)
-    for where in (sibling, to_up, to_down):
+    for where in (sibling, {"head": near[0]}, {"head": near[1]}):
         pl.semaphore_signal(barrier, inc=1, device_id=where, device_id_type=MESH)
-    load_k.wait()
-    load_v.wait()
+    for copy in [load_k, load_v] + load_w + [load_cot, load_q]:
+        copy.wait()
     pl.semaphore_wait(barrier, chips - 1 + 3)
+
+    wx_rows = wx.shape[2]
+    blocks = chips // 2
+    giver = near[0] + core * (near[1] - near[0])
+    opposite = groups - 1 - near[0]
+    block = lax.div(me, blocks)
+    column = giver + block * (opposite - giver)
+    row = pl.ds(pl.multiple_of(lax.rem(me, blocks) * wx_rows, wx_rows), wx_rows)
+    wx_cross = remote(
+        w.at[column, row], wx.at[core, me], wx_send.at[0], wx_recv.at[0], {"head": giver}
+    )
+    wx_cross.start()
+    units, side = digits(chips)
+
+    def wx_stage(axis):
+        unit = units[axis]
+        digit = lax.rem(lax.div(me, unit), side)
+        have = wx.at[core, pl.ds(lax.div(me, unit) * unit, unit)]
+        for j in range(1, side):
+            p = me + (lax.rem(digit + j, side) - digit) * unit
+            remote(have, have, wx_send.at[1 + axis], wx_recv.at[1 + axis], on_chip(p)).start()
+
+    def wx_stage_span(axis):
+        return wx.at[core, pl.ds(0, (side - 1) * units[axis])]
 
     def spread(src, dst, phase):
         def body(step, carry):
@@ -119,34 +147,43 @@
     def all_arrived(dst, phase):
         arrived(dst.at[pl.ds(0, chips - 1)], a2a_recv.at[phase])
 
+    def to_near(src, dst, slot, side):
+        return remote(src, dst, hd_send.at[slot], hd_recv.at[slot], {"head": near[side]})
+
     spread(kv.at[0], in1, 0)
     swap_own = remote(kv.at[0], kv.at[1], pair_send.at[0], pair_recv.at[0], sibling)
     swap_own.start()
-
-    load_cot.wait()
-    lo, top = pl.ds(0, mid), pl.ds(mid, mid)
-    ag_up = [
-        remote(cot.at[hi, s], cot.at[hi, s], ag_send.at[i], ag_recv.at[i], to_up)
-        for i, s in enumerate((lo, top))
-    ]
-    ag_down = [
-        remote(cot.at[hi, s], cot.at[hi, s], ag_send.at[2 + i], ag_recv.at[2 + i], to_down)
-        for i, s in enumerate((top, lo))
-    ]
-    for copy in (ag_up[0], ag_down[0], ag_up[1], ag_down[1]):
+    cot_swap = [to_near(cot.at[side_rows[t]], cot_m.at[t], t, t) for t in range(2)]
+    for copy in cot_swap:
         copy.start()
 
+    wx_cross.wait_recv()
+    wx_stage(2)
+    arrived(wx_stage_span(2), wx_recv.at[3])
+    wx_stage(1)
     all_arrived(in1, 0)
     forward(in1, perm_ref, out1, kv.at[2], 1)
-
-    ag_up[0].wait_recv()
-    pass_up = remote(cot.at[down, lo], cot.at[down, lo], ag_send.at[4], ag_recv.at[4], to_up)
-    pass_up.start()
-    ag_down[0].wait_recv()
-    pass_down = remote(cot.at[up, top], cot.at[up, top], ag_send.at[5], ag_recv.at[5], to_down)
-    pass_down.start()
-
-    load_q.wait()
+    arrived(wx_stage_span(1), wx_recv.at[2])
+    wx_stage(0)
+
+    def neighbour_w(source, which):
+        return wx[source, pl.ds(which * blocks, blocks)].reshape(blocks * wx_rows, cols)
+
+    for t in range(2):
+        cot_swap[t].wait_recv()
+        g_acc[t] = nt(cot[side_rows[t]], w[hi]) + nt(cot_m[t], w[near[t]])
+
+    arrived(wx_stage_span(0), wx_recv.at[1])
+    swap_wx = remote(wx.at[core], wx.at[core], pair_send.at[4], pair_recv.at[4], sibling)
+    swap_wx.start()
+    swap_wx.wait_recv()
+    gp_swap = []
+    for t in range(2):
+        both = nt(cot[side_rows[t]], neighbour_w(1 - t, 0)) + nt(cot_m[t], neighbour_w(1 - t, 1))
+        gp_out[t] = both.astype(BF)
+        gp_swap.append(to_near(gp_out.at[t], gp_in.at[t], 2 + t, 1 - t))
+        gp_swap[t].start()
+
     all_arrived(kv.at[2], 1)
     swap_partner = remote(kv.at[2], kv.at[3], pair_send.at[1], pair_recv.at[1], sibling)
     swap_partner.start()
@@ -176,56 +213,26 @@
             acc = term if acc is None else acc + term
         low = acc.astype(BF)
         att_t[h] = low
-        att[h] = low.T
+        att[:, pl.ds(pl.multiple_of(h * width, width), width)] = low.T
         return carry
 
     lax.fori_loop(0, heads, attend, 0)
 
-    for copy in load_w:
-        copy.wait()
-
-    def project(c):
-        acc = None
+    att_swap = [to_near(att.at[side_rows[t]], att_m.at[t], 4 + t, t) for t in range(2)]
+    for copy in att_swap:
+        copy.start()
+
+    for t in range(2):
+        gp_swap[t].wait_recv()
+        both = (g_acc[t] + gp_in[t].astype(F32)).astype(BF)
         for h in range(heads):
-            term = nn(att[h], w[c, pl.ds(h * width, width)])
-            acc = term if acc is None else acc + term
-        part[c] = acc.astype(BF)
-
-    project(far)
-    rs_a = remote(part.at[far, lo], rs_far.at[0], rs_send.at[0], rs_recv.at[0], to_up)
-    rs_b = remote(part.at[far, top], rs_far.at[1], rs_send.at[1], rs_recv.at[1], to_down)
-    rs_a.start()
-    rs_b.start()
-    project(up)
-    rs_c = remote(part.at[up, top], rs_near.at[0, top], rs_send.at[2], rs_recv.at[2], to_up)
-    rs_c.start()
-    project(down)
-    rs_d = remote(part.at[down, lo], rs_near.at[1, lo], rs_send.at[3], rs_recv.at[3], to_down)
-    rs_d.start()
-    project(hi)
-
-    ag_up[1].wait_recv()
-    ag_down[1].wait_recv()
-    pass_up.wait_recv()
-    pass_down.wait_recv()
-
-    def pull(h, carry):
-        acc = None
-        for c in range(groups):
-            term = nt(cot[c], w[c, pl.ds(pl.multiple_of(h * width, width), width)])
-            acc = term if acc is None else acc + term
-        low = acc.astype(BF)
-        grad[h] = low
-        grad_t[h] = low.T
-        return carry
-
-    lax.fori_loop(0, heads, pull, 0)
+            grad[h, side_rows[t]] = both[:, h * width:(h + 1) * width]
 
     def differentiate(h, carry):
         q_h = q[h]
         grad_h = grad[h]
         delta = jnp.sum(
-            grad_t[h].astype(F32) * att_t[h].astype(F32), axis=0, keepdims=True
+            grad_h.T.astype(F32) * att_t[h].astype(F32), axis=0, keepdims=True
         )
         dq_t = None
         for slot in range(4):
@@ -253,29 +260,28 @@
     swap_term.start()
     swap_pair.start()
     swap_term.wait_recv()
-    both = give[1].astype(F32) + got[1].astype(F32)
-    give[1] = both.astype(BF)
+    both_cores = give[1].astype(F32) + got[1].astype(F32)
+    give[1] = both_cores.astype(BF)
 
     spread(give.at[1], in3, 2)
 
-    rs_a.wait_recv()
-    part[up, lo] = (part[up, lo].astype(F32) + rs_far[0].astype(F32)).astype(BF)
-    rs_e = remote(part.at[up, lo], rs_near.at[0, lo], rs_send.at[4], rs_recv.at[4], to_up)
-    rs_e.start()
-    rs_b.wait_recv()
-    part[down, top] = (part[down, top].astype(F32) + rs_far[1].astype(F32)).astype(BF)
-    rs_f = remote(part.at[down, top], rs_near.at[1, top], rs_send.at[5], rs_recv.at[5], to_down)
-    rs_f.start()
+    pp_swap = []
+    for t in range(2):
+        att_swap[t].wait_recv()
+        both = nn(att[side_rows[t]], w[near[1 - t]]) + nn(att_m[t], neighbour_w(t, 1))
+        pp_out[t] = both.astype(BF)
+        pp_swap.append(to_near(pp_out.at[t], pp_in.at[t], 6 + t, 1 - t))
+        pp_swap[t].start()
+    for t in range(2):
+        g_acc[t] = nn(att[side_rows[t]], w[hi]) + nn(att_m[t], neighbour_w(t, 0))
 
     all_arrived(in3, 2)
     forward(in3, inv_ref, out3, back, 3)
 
     swap_pair.wait_recv()
-    for copy in (rs_c, rs_d, rs_e, rs_f):
-        copy.wait_recv()
-    proj_ref[...] = (
-        part[hi].astype(F32) + rs_near[0].astype(F32) + rs_near[1].astype(F32)
-    ).astype(BF)
+    for t in range(2):
+        pp_swap[t].wait_recv()
+        proj_ref[side_rows[t]] = (g_acc[t] + pp_in[t].astype(F32)).astype(BF)
 
     all_arrived(back, 3)
 
@@ -291,9 +297,11 @@
 
     for phase, ref in enumerate((kv.at[0], out1, give.at[1], out3)):
         arrived(ref.at[pl.ds(0, chips - 1)], a2a_send.at[phase])
+    for axis in range(3):
+        arrived(wx_stage_span(axis), wx_send.at[1 + axis])
     for copy in (
-        [swap_own, swap_partner, swap_pair, swap_term, pass_up, pass_down]
-        + ag_up + ag_down + [rs_a, rs_b, rs_c, rs_d, rs_e, rs_f]
+        [swap_own, swap_partner, swap_pair, swap_term, swap_wx, wx_cross]
+        + cot_swap + gp_swap + att_swap + pp_swap
     ):
         copy.wait_send()
 
@@ -308,43 +316,49 @@
     inverse = jnp.sum(
         jnp.where(block_perm[:, None, :] == blocks[None, :, None], blocks[None, None, :], 0), axis=2
     )
-    any_space = pl.BlockSpec(memory_space=pl.ANY)
+    in_hbm = pl.BlockSpec(memory_space=pltpu.HBM)
     smem = pl.BlockSpec(memory_space=pltpu.SMEM)
     vmem = pl.BlockSpec(memory_space=pltpu.VMEM)
     mat = jax.ShapeDtypeStruct((heads, tok, width), BF)
     pieces = (chips, rows, width)
+    sides = (2, tok // 2, cols)
+    flat = heads * width
     dma = pltpu.SemaphoreType.DMA
     scratch = [
         pltpu.VMEM((4,) + pieces, BF),
         pltpu.VMEM((heads, tok, width), BF),
-        pltpu.VMEM((groups, heads * width, cols), BF),
-        pltpu.VMEM((groups, tok, cols), BF),
+        pltpu.VMEM((groups, flat, cols), BF),
+        pltpu.VMEM((2, chips, 2 * flat // chips, cols), BF),
+        pltpu.VMEM((tok, cols), BF),
+        pltpu.VMEM(sides, BF),
+        pltpu.VMEM((2, tok // 2, flat), BF),
+        pltpu.VMEM((2, tok // 2, flat), BF),
+        pltpu.VMEM((2, tok // 2, max(flat, cols)), F32),
         pltpu.VMEM(pieces, BF),
         pltpu.VMEM(pieces, BF),
         pltpu.VMEM(pieces, BF),
         pltpu.VMEM(pieces, BF),
         pltpu.VMEM(pieces, BF),
         pltpu.VMEM((heads, 4, tok, tok), BF),
+        pltpu.VMEM((tok, flat), BF),
+        pltpu.VMEM((2, tok // 2, flat), BF),
+        pltpu.VMEM((heads, width, tok), BF),
         pltpu.VMEM((heads, tok, width), BF),
-        pltpu.VMEM((heads, tok, width), BF),
-        pltpu.VMEM((heads, width, tok), BF),
-        pltpu.VMEM((heads, width, tok), BF),
+        pltpu.VMEM(sides, BF),
+        pltpu.VMEM(sides, BF),
         pltpu.VMEM(pieces, F32),
         pltpu.VMEM((3,) + pieces, BF),
         pltpu.VMEM((2,) + pieces, BF),
-        pltpu.VMEM((groups, tok, cols), BF),
-        pltpu.VMEM((2, tok // 2, cols), BF),
-        pltpu.VMEM((2, tok, cols), BF),
-        dma((8,)), dma((4,)), dma((4,)), dma((4,)), dma((4,)), dma((6,)), dma((6,)), dma((6,)), dma((6,)),
+        dma((8,)), dma((4,)), dma((4,)), dma((5,)), dma((5,)), dma((4,)), dma((4,)), dma((8,)), dma((8,)),
     ]
     return pl.pallas_call(
         functools.partial(kernel, (heads, tok, width, chips, groups)),
         out_shape=(jax.ShapeDtypeStruct((tok, cols), BF), mat, mat, mat),
-        in_specs=[smem, smem] + [any_space] * 5,
+        in_specs=[smem, smem] + [in_hbm] * 5,
         out_specs=(vmem,) * 4,
         scratch_shapes=scratch,
         compiler_params=pltpu.CompilerParams(
-            collective_id=0, has_side_effects=True, vmem_limit_bytes=48 << 20
+            collective_id=0, has_side_effects=True, vmem_limit_bytes=60 << 20
         ),
     )(
         block_perm,

time: 151 us -> 143 us (0.947)
  Pallas kernels: 140 us -> 134 us
  local copies, waits for them, and re-layouts: 8.88 us -> 6.68 us
    pallas_call x1, Pallas kernels: 140 us -> 134 us  [per_device(): pl.pallas_call(functools.partial(kernel, (heads, tok, width, chips, group...]
    unnamed x16 -> x4, local copies, waits for them, and re-layouts: 8.88 us -> 6.68 us
where the time goes in v2:
time: 143 us
  Pallas kernels  134 us (94%)
  local copies, waits for them, and re-layouts  6.68 us (5%)
    pallas_call x1, Pallas kernels, per_device(): pl.pallas_call(functools.partial(kernel, (heads, tok, width, chips, group...  134 us
    unnamed x4, local copies, waits for them, and re-layouts  6.68 us

profile of v2, /device:TPU:1, one launch (start us, length us, event | category | flops | bytes accessed | tf_op | source)
XLA Modules:
  0.0 142.6 jit_solution(16310736658788236324)
XLA Ops:
  0.6 1.4 select_reduce_fusion.inv_ref
  2.0 133.9 %shard_map.93 = (bf16[256,512]{1,0:T(8,128)(2,1)}, bf16[4,256,128]{2,1,0:T(8,128)(2,1)}, bf16[4,256,128]{2,1,0:T(8,128)(2,1)}, bf16[4,256,128]{2,1,0:T(8,128)(2,1)}) custom-call(s32[4,64]{1,0:T(4,128)} %perm_ref.1, s32[4,64]{1,0:T(4,128)} %select_reduce_fusion.inv_ref, bf16[4,256,128]{2,1,0:T(8,128)(2,1)} %q_hbm.1, bf16[32,32,128]{2,1,0:T(8,128)(2,1)} %bitcast.4, ...), custom_call_target="tpu_custom_call" | custom-call | tf_op jit(solution)/shard_map/pallas_call | solution.py:354
  136.0 1.7 %copy.14 = bf16[256,512]{1,0:T(8,128)(2,1)} copy(bf16[256,512]{1,0:T(8,128)(2,1)} %get-tuple-element.8) | data formatting | bytes 524288
  137.6 1.7 %copy.15 = bf16[4,256,128]{2,1,0:T(8,128)(2,1)} copy(bf16[4,256,128]{2,1,0:T(8,128)(2,1)} %get-tuple-element.9) | data formatting | bytes 524288
  139.3 1.7 %copy.16 = bf16[4,256,128]{2,1,0:T(8,128)(2,1)} copy(bf16[4,256,128]{2,1,0:T(8,128)(2,1)} %get-tuple-element.10) | data formatting | bytes 524288
  141.0 1.7 %copy.17 = bf16[4,256,128]{2,1,0:T(8,128)(2,1)} copy(bf16[4,256,128]{2,1,0:T(8,128)(2,1)} %get-tuple-element.11) | data formatting | bytes 524288

commit v3 on v2

--- a/solution.py
+++ b/solution.py
@@ -41,9 +41,9 @@
 
 def kernel(
     dims,
-    perm_ref, inv_ref, q_hbm, k_hbm, v_hbm, w_hbm, cot_hbm,
+    perm_ref, q_hbm, k_hbm, v_hbm, w_hbm, cot_hbm,
     proj_ref, dq_ref, dk_ref, dv_ref,
-    kv, q, w, wx, cot, cot_m, gp_out, gp_in, g_acc,
+    inv_row, inv_ref, kv, q, w, wx, cot, cot_m, gp_out, gp_in, g_acc,
     in1, out1, in3, out3, back, prob, att, att_m, att_t, grad, pp_out, pp_in,
     own, give, got,
     load_sem, a2a_send, a2a_recv, pair_send, pair_recv, wx_send, wx_recv, hd_send, hd_recv,
@@ -101,29 +101,53 @@
         copy.wait()
     pl.semaphore_wait(barrier, chips - 1 + 3)
 
-    wx_rows = wx.shape[2]
+    units, edge = digits(chips)
+    x, y, z = (lax.rem(lax.div(me, unit), edge) for unit in units)
+    wx_rows = wx.shape[4]
     blocks = chips // 2
     giver = near[0] + core * (near[1] - near[0])
     opposite = groups - 1 - near[0]
     block = lax.div(me, blocks)
     column = giver + block * (opposite - giver)
     row = pl.ds(pl.multiple_of(lax.rem(me, blocks) * wx_rows, wx_rows), wx_rows)
+    mine = wx.at[core]
     wx_cross = remote(
-        w.at[column, row], wx.at[core, me], wx_send.at[0], wx_recv.at[0], {"head": giver}
+        w.at[column, row], mine.at[x, y, z], wx_send.at[0], wx_recv.at[0], {"head": giver}
     )
     wx_cross.start()
-    units, side = digits(chips)
-
-    def wx_stage(axis):
-        unit = units[axis]
-        digit = lax.rem(lax.div(me, unit), side)
-        have = wx.at[core, pl.ds(lax.div(me, unit) * unit, unit)]
-        for j in range(1, side):
-            p = me + (lax.rem(digit + j, side) - digit) * unit
-            remote(have, have, wx_send.at[1 + axis], wx_recv.at[1 + axis], on_chip(p)).start()
-
-    def wx_stage_span(axis):
-        return wx.at[core, pl.ds(0, (side - 1) * units[axis])]
+
+    def wx_share(have, axis, sem):
+        unit, digit = units[axis], (x, y, z)[axis]
+        for j in range(1, edge):
+            p = me + (lax.rem(digit + j, edge) - digit) * unit
+            remote(have, have, wx_send.at[sem], wx_recv.at[sem], on_chip(p)).start()
+
+    low_z, high_z = pl.ds(0, edge // 2), pl.ds(edge // 2, edge // 2)
+    others = pl.ds(0, edge - 1)
+    wx_spans = (
+        mine.at[0, 0, others],
+        mine.at[0, others, low_z], mine.at[others, 0, low_z],
+        mine.at[others, :, low_z], mine.at[:, others, low_z],
+    )
+
+    def wx_wait(sems, index):
+        for sem in index:
+            arrived(wx_spans[sem - 1], sems.at[sem])
+
+    def wx_start():
+        wx_share(mine.at[x, y, z], 2, 1)
+
+    def wx_first():
+        wx_wait(wx_recv, (1,))
+        wx_share(mine.at[x, y, low_z], 1, 2)
+        wx_share(mine.at[x, y, high_z], 0, 3)
+
+    def wx_end_first():
+        wx_wait(wx_recv, (2, 3))
+
+    def wx_second():
+        wx_share(mine.at[x, :, low_z], 0, 4)
+        wx_share(mine.at[:, y, high_z], 1, 5)
 
     def spread(src, dst, phase):
         def body(step, carry):
@@ -134,15 +158,26 @@
         lax.fori_loop(1, chips, body, 0)
         dst[me] = src[me]
 
-    def forward(src, table, out, dst, phase):
+    def forward(src, table, row, out, dst, phase):
         def body(step, carry):
             p = peer_chip(me, step, chips)
-            out[p] = src[table[my_head, p]]
+            out[p] = src[table[row, p]]
             remote(out.at[p], dst.at[me], a2a_send.at[phase], a2a_recv.at[phase], on_chip(p)).start()
             return carry
 
         lax.fori_loop(1, chips, body, 0)
-        dst[me] = src[table[my_head, me]]
+        dst[me] = src[table[row, me]]
+
+    def invert():
+        lane = lax.broadcasted_iota(jnp.int32, (8, 128), 1)
+
+        def body(b, row):
+            return jnp.where(lane == perm_ref[my_head, b], b, row)
+
+        inv_row[...] = lax.fori_loop(0, chips, body, jnp.zeros((8, 128), jnp.int32))
+        copy = pltpu.make_async_copy(inv_row, inv_ref, load_sem.at[8])
+        copy.start()
+        copy.wait()
 
     def all_arrived(dst, phase):
         arrived(dst.at[pl.ds(0, chips - 1)], a2a_recv.at[phase])
@@ -151,29 +186,30 @@
         return remote(src, dst, hd_send.at[slot], hd_recv.at[slot], {"head": near[side]})
 
     spread(kv.at[0], in1, 0)
+    wx_cross.wait_recv()
+    wx_start()
     swap_own = remote(kv.at[0], kv.at[1], pair_send.at[0], pair_recv.at[0], sibling)
     swap_own.start()
     cot_swap = [to_near(cot.at[side_rows[t]], cot_m.at[t], t, t) for t in range(2)]
     for copy in cot_swap:
         copy.start()
 
-    wx_cross.wait_recv()
-    wx_stage(2)
-    arrived(wx_stage_span(2), wx_recv.at[3])
-    wx_stage(1)
+    wx_first()
     all_arrived(in1, 0)
-    forward(in1, perm_ref, out1, kv.at[2], 1)
-    arrived(wx_stage_span(1), wx_recv.at[2])
-    wx_stage(0)
+    forward(in1, perm_ref, my_head, out1, kv.at[2], 1)
+    wx_end_first()
+    wx_second()
+    invert()
 
     def neighbour_w(source, which):
-        return wx[source, pl.ds(which * blocks, blocks)].reshape(blocks * wx_rows, cols)
+        value = wx[source, pl.ds(which * (edge // 2), edge // 2)]
+        return value.reshape(blocks * wx_rows, cols)
 
     for t in range(2):
         cot_swap[t].wait_recv()
         g_acc[t] = nt(cot[side_rows[t]], w[hi]) + nt(cot_m[t], w[near[t]])
 
-    arrived(wx_stage_span(0), wx_recv.at[1])
+    wx_wait(wx_recv, (4, 5))
     swap_wx = remote(wx.at[core], wx.at[core], pair_send.at[4], pair_recv.at[4], sibling)
     swap_wx.start()
     swap_wx.wait_recv()
@@ -276,7 +312,7 @@
         g_acc[t] = nn(att[side_rows[t]], w[hi]) + nn(att_m[t], neighbour_w(t, 0))
 
     all_arrived(in3, 2)
-    forward(in3, inv_ref, out3, back, 3)
+    forward(in3, inv_ref, 0, out3, back, 3)
 
     swap_pair.wait_recv()
     for t in range(2):
@@ -297,13 +333,17 @@
 
     for phase, ref in enumerate((kv.at[0], out1, give.at[1], out3)):
         arrived(ref.at[pl.ds(0, chips - 1)], a2a_send.at[phase])
-    for axis in range(3):
-        arrived(wx_stage_span(axis), wx_send.at[1 + axis])
+    wx_wait(wx_send, (1, 2, 3, 4, 5))
     for copy in (
         [swap_own, swap_partner, swap_pair, swap_term, swap_wx, wx_cross]
         + cot_swap + gp_swap + att_swap + pp_swap
     ):
         copy.wait_send()
+
+
+def hand_out(*refs):
+    for source, target in zip(refs[:4], refs[4:]):
+        target[...] = source[...]
 
 
 def per_device(queries, key_vectors, value_vectors, block_perm, out_weight, out_cotangent):
@@ -312,10 +352,6 @@
     heads, tok, width = queries.shape
     rows = 2 * heads * tok // chips
     cols = out_cotangent.shape[1]
-    blocks = lax.iota(jnp.int32, chips)
-    inverse = jnp.sum(
-        jnp.where(block_perm[:, None, :] == blocks[None, :, None], blocks[None, None, :], 0), axis=2
-    )
     in_hbm = pl.BlockSpec(memory_space=pltpu.HBM)
     smem = pl.BlockSpec(memory_space=pltpu.SMEM)
     vmem = pl.BlockSpec(memory_space=pltpu.VMEM)
@@ -323,12 +359,15 @@
     pieces = (chips, rows, width)
     sides = (2, tok // 2, cols)
     flat = heads * width
+    edge = digits(chips)[1]
     dma = pltpu.SemaphoreType.DMA
     scratch = [
+        pltpu.VMEM((8, 128), jnp.int32),
+        pltpu.SMEM((8, 128), jnp.int32),
         pltpu.VMEM((4,) + pieces, BF),
         pltpu.VMEM((heads, tok, width), BF),
         pltpu.VMEM((groups, flat, cols), BF),
-        pltpu.VMEM((2, chips, 2 * flat // chips, cols), BF),
+        pltpu.VMEM((2, edge, edge, edge, 2 * flat // chips, cols), BF),
         pltpu.VMEM((tok, cols), BF),
         pltpu.VMEM(sides, BF),
         pltpu.VMEM((2, tok // 2, flat), BF),
@@ -349,12 +388,12 @@
         pltpu.VMEM(pieces, F32),
         pltpu.VMEM((3,) + pieces, BF),
         pltpu.VMEM((2,) + pieces, BF),
-        dma((8,)), dma((4,)), dma((4,)), dma((5,)), dma((5,)), dma((4,)), dma((4,)), dma((8,)), dma((8,)),
+        dma((9,)), dma((4,)), dma((4,)), dma((5,)), dma((5,)), dma((6,)), dma((6,)), dma((8,)), dma((8,)),
     ]
-    return pl.pallas_call(
+    results = pl.pallas_call(
         functools.partial(kernel, (heads, tok, width, chips, groups)),
         out_shape=(jax.ShapeDtypeStruct((tok, cols), BF), mat, mat, mat),
-        in_specs=[smem, smem] + [in_hbm] * 5,
+        in_specs=[smem] + [in_hbm] * 5,
         out_specs=(vmem,) * 4,
         scratch_shapes=scratch,
         compiler_params=pltpu.CompilerParams(
@@ -362,13 +401,19 @@
         ),
     )(
         block_perm,
-        inverse,
         queries,
         key_vectors.reshape(chips // 2, rows, width),
         value_vectors.reshape(chips // 2, rows, width),
         out_weight.reshape(heads * width, -1),
         out_cotangent,
     )
+    shapes = (jax.ShapeDtypeStruct((tok, cols), BF), mat, mat, mat)
+    return pl.pallas_call(
+        hand_out,
+        out_shape=shapes,
+        in_specs=[vmem] * 4,
+        out_specs=(vmem,) * 4,
+    )(*results)
 
 
 def solution(mesh):

time: 143 us -> 128 us (0.90)
  Pallas kernels: 134 us -> 126 us
  local copies, waits for them, and re-layouts: 6.68 us -> 0 us
    pallas_call x1, Pallas kernels: 134 us -> 124 us  [per_device(): pl.pallas_call(functools.partial(kernel, (heads, tok, width, chips, group...]
    unnamed x4 -> x0, local copies, waits for them, and re-layouts: 6.68 us -> none
    pallas_call x0 -> x1, Pallas kernels: none -> 2.17 us  [per_device(): pl.pallas_call(hand_out, out_shape=shapes, in_specs=[vmem] * 4, out_specs...]
where the time goes in v3:
time: 128 us; the launch traced here: 127 us
  Pallas kernels  126 us (98%)
    pallas_call x1, Pallas kernels, per_device(): pl.pallas_call(functools.partial(kernel, (heads, tok, width, chips, group...  124 us

profile of v3, /device:TPU:1, one launch (start us, length us, event | category | flops | bytes accessed | tf_op | source)
XLA Modules:
  0.0 127.1 jit_solution(6604212904785731033)
XLA Ops:
  0.6 124.3 %shard_map.93 = (bf16[256,512]{1,0:T(8,128)(2,1)}, bf16[4,256,128]{2,1,0:T(8,128)(2,1)}, bf16[4,256,128]{2,1,0:T(8,128)(2,1)}, bf16[4,256,128]{2,1,0:T(8,128)(2,1)}) custom-call(s32[4,64]{1,0:T(4,128)} %perm_ref.1, bf16[4,256,128]{2,1,0:T(8,128)(2,1)} %q_hbm.1, bf16[32,32,128]{2,1,0:T(8,128)(2,1)} %bitcast.4, bf16[32,32,128]{2,1,0:T(8,128)(2,1)} %bitcast.5, ...), custom_call_target="tpu_custom_call" | custom-call | tf_op jit(solution)/shard_map/pallas_call | solution.py:393
  124.9 2.2 %shard_map.94 = (bf16[256,512]{1,0:T(8,128)(2,1)}, bf16[4,256,128]{2,1,0:T(8,128)(2,1)}, bf16[4,256,128]{2,1,0:T(8,128)(2,1)}, bf16[4,256,128]{2,1,0:T(8,128)(2,1)}) custom-call(bf16[256,512]{1,0:T(8,128)(2,1)} %get-tuple-element.8.refs_0_, bf16[4,256,128]{2,1,0:T(8,128)(2,1)} %get-tuple-element.9.refs_1_, bf16[4,256,128]{2,1,0:T(8,128)(2,1)} %get-tuple-element.10.refs_2_, ...), custom_call_target="tpu_custom_call" | custom-call | tf_op jit(solution)/shard_map/pallas_call | solution.py:411

commit v4 on v3

--- a/solution.py
+++ b/solution.py
@@ -191,12 +191,12 @@
     swap_own = remote(kv.at[0], kv.at[1], pair_send.at[0], pair_recv.at[0], sibling)
     swap_own.start()
     cot_swap = [to_near(cot.at[side_rows[t]], cot_m.at[t], t, t) for t in range(2)]
-    for copy in cot_swap:
-        copy.start()
-
+
+    cot_swap[0].start()
     wx_first()
     all_arrived(in1, 0)
     forward(in1, perm_ref, my_head, out1, kv.at[2], 1)
+    cot_swap[1].start()
     wx_end_first()
     wx_second()
     invert()
@@ -212,6 +212,9 @@
     wx_wait(wx_recv, (4, 5))
     swap_wx = remote(wx.at[core], wx.at[core], pair_send.at[4], pair_recv.at[4], sibling)
     swap_wx.start()
+    all_arrived(kv.at[2], 1)
+    swap_partner = remote(kv.at[2], kv.at[3], pair_send.at[1], pair_recv.at[1], sibling)
+    swap_partner.start()
     swap_wx.wait_recv()
     gp_swap = []
     for t in range(2):
@@ -220,9 +223,6 @@
         gp_swap.append(to_near(gp_out.at[t], gp_in.at[t], 2 + t, 1 - t))
         gp_swap[t].start()
 
-    all_arrived(kv.at[2], 1)
-    swap_partner = remote(kv.at[2], kv.at[3], pair_send.at[1], pair_recv.at[1], sibling)
-    swap_partner.start()
     swap_own.wait_recv()
     swap_partner.wait_recv()
 

time: 128 us -> 124 us (0.969)
  Pallas kernels: 126 us -> 123 us
    pallas_call x1, Pallas kernels: 124 us -> 120 us  [per_device(): pl.pallas_call(functools.partial(kernel, (heads, tok, width, chips, group...]
where the time goes in v4:
time: 124 us; the launch traced here: 123 us
  Pallas kernels  123 us (99%)
    pallas_call x1, Pallas kernels, per_device(): pl.pallas_call(functools.partial(kernel, (heads, tok, width, chips, group...  120 us

profile of v4, /device:TPU:1, one launch (start us, length us, event | category | flops | bytes accessed | tf_op | source)
XLA Modules:
  0.0 123.3 jit_solution(3564963007832331979)
XLA Ops:
  0.6 120.5 %shard_map.93 = (bf16[256,512]{1,0:T(8,128)(2,1)}, bf16[4,256,128]{2,1,0:T(8,128)(2,1)}, bf16[4,256,128]{2,1,0:T(8,128)(2,1)}, bf16[4,256,128]{2,1,0:T(8,128)(2,1)}) custom-call(s32[4,64]{1,0:T(4,128)} %perm_ref.1, bf16[4,256,128]{2,1,0:T(8,128)(2,1)} %q_hbm.1, bf16[32,32,128]{2,1,0:T(8,128)(2,1)} %bitcast.4, bf16[32,32,128]{2,1,0:T(8,128)(2,1)} %bitcast.5, ...), custom_call_target="tpu_custom_call" | custom-call | tf_op jit(solution)/shard_map/pallas_call | solution.py:393
  121.1 2.2 %shard_map.94 = (bf16[256,512]{1,0:T(8,128)(2,1)}, bf16[4,256,128]{2,1,0:T(8,128)(2,1)}, bf16[4,256,128]{2,1,0:T(8,128)(2,1)}, bf16[4,256,128]{2,1,0:T(8,128)(2,1)}) custom-call(bf16[256,512]{1,0:T(8,128)(2,1)} %get-tuple-element.8.refs_0_, bf16[4,256,128]{2,1,0:T(8,128)(2,1)} %get-tuple-element.9.refs_1_, bf16[4,256,128]{2,1,0:T(8,128)(2,1)} %get-tuple-element.10.refs_2_, ...), custom_call_target="tpu_custom_call" | custom-call | tf_op jit(solution)/shard_map/pallas_call | solution.py:411

commit v5 on v4

--- a/solution.py
+++ b/solution.py
@@ -45,7 +45,7 @@
     proj_ref, dq_ref, dk_ref, dv_ref,
     inv_row, inv_ref, kv, q, w, wx, cot, cot_m, gp_out, gp_in, g_acc,
     in1, out1, in3, out3, back, prob, att, att_m, att_t, grad, pp_out, pp_in,
-    own, give, got,
+    own, give, got, dq_acc,
     load_sem, a2a_send, a2a_recv, pair_send, pair_recv, wx_send, wx_recv, hd_send, hd_recv,
 ):
     heads, tok, width, chips, groups = dims
@@ -264,14 +264,14 @@
         for h in range(heads):
             grad[h, side_rows[t]] = both[:, h * width:(h + 1) * width]
 
-    def differentiate(h, carry):
+    def differentiate(h, slots):
         q_h = q[h]
         grad_h = grad[h]
         delta = jnp.sum(
             grad_h.T.astype(F32) * att_t[h].astype(F32), axis=0, keepdims=True
         )
         dq_t = None
-        for slot in range(4):
+        for slot in slots:
             low = prob[h, slot]
             d_prob = nt(rows_of(slot, 1, h), grad_h)
             d_score = (low.astype(F32) * ((d_prob - delta) * scale)).astype(BF)
@@ -286,20 +286,31 @@
                     own[where] = value
                 else:
                     give[slot - 1, where] = value.astype(BF)
+        return dq_t
+
+    def partner_rows(h, carry):
+        dq_acc[h] = differentiate(h, (3, 2))
+        for which in range(2):
+            where = pl.ds((which * heads + h) * per_head, per_head)
+            remote(
+                give.at[2, where], got.at[1, where], pair_send.at[3], pair_recv.at[3], sibling
+            ).start()
+        return carry
+
+    def block_rows(h, carry):
+        dq_t = dq_acc[h] + differentiate(h, (1, 0))
         dq_ref[h] = dq_t.T.astype(BF)
         return carry
 
-    lax.fori_loop(0, heads, differentiate, 0)
-
+    lax.fori_loop(0, heads, partner_rows, 0)
     swap_pair = remote(give.at[0], got.at[0], pair_send.at[2], pair_recv.at[2], sibling)
-    swap_term = remote(give.at[2], got.at[1], pair_send.at[3], pair_recv.at[3], sibling)
-    swap_term.start()
-    swap_pair.start()
-    swap_term.wait_recv()
+    arrived(got.at[1], pair_recv.at[3])
     both_cores = give[1].astype(F32) + got[1].astype(F32)
     give[1] = both_cores.astype(BF)
 
     spread(give.at[1], in3, 2)
+    lax.fori_loop(0, heads, block_rows, 0)
+    swap_pair.start()
 
     pp_swap = []
     for t in range(2):
@@ -331,11 +342,12 @@
 
     lax.fori_loop(0, heads, finish, 0)
 
+    arrived(give.at[2], pair_send.at[3])
     for phase, ref in enumerate((kv.at[0], out1, give.at[1], out3)):
         arrived(ref.at[pl.ds(0, chips - 1)], a2a_send.at[phase])
     wx_wait(wx_send, (1, 2, 3, 4, 5))
     for copy in (
-        [swap_own, swap_partner, swap_pair, swap_term, swap_wx, wx_cross]
+        [swap_own, swap_partner, swap_pair, swap_wx, wx_cross]
         + cot_swap + gp_swap + att_swap + pp_swap
     ):
         copy.wait_send()
@@ -388,6 +400,7 @@
         pltpu.VMEM(pieces, F32),
         pltpu.VMEM((3,) + pieces, BF),
         pltpu.VMEM((2,) + pieces, BF),
+        pltpu.VMEM((heads, width, tok), F32),
         dma((9,)), dma((4,)), dma((4,)), dma((5,)), dma((5,)), dma((6,)), dma((6,)), dma((8,)), dma((8,)),
     ]
     results = pl.pallas_call(

time: 124 us -> 123 us (level)
  no operation moved by 1% of the time
where the time goes in v5:
time: 123 us
  Pallas kernels  122 us (99%)
    pallas_call x1, Pallas kernels, per_device(): pl.pallas_call(functools.partial(kernel, (heads, tok, width, chips, group...  120 us

profile of v5, /device:TPU:1, one launch (start us, length us, event | category | flops | bytes accessed | tf_op | source)
XLA Modules:
  0.0 122.8 jit_solution(15999242697428710665)
XLA Ops:
  0.6 119.9 %shard_map.93 = (bf16[256,512]{1,0:T(8,128)(2,1)}, bf16[4,256,128]{2,1,0:T(8,128)(2,1)}, bf16[4,256,128]{2,1,0:T(8,128)(2,1)}, bf16[4,256,128]{2,1,0:T(8,128)(2,1)}) custom-call(s32[4,64]{1,0:T(4,128)} %perm_ref.1, bf16[4,256,128]{2,1,0:T(8,128)(2,1)} %q_hbm.1, bf16[32,32,128]{2,1,0:T(8,128)(2,1)} %bitcast.4, bf16[32,32,128]{2,1,0:T(8,128)(2,1)} %bitcast.5, ...), custom_call_target="tpu_custom_call" | custom-call | tf_op jit(solution)/shard_map/pallas_call | solution.py:406
  120.6 2.2 %shard_map.94 = (bf16[256,512]{1,0:T(8,128)(2,1)}, bf16[4,256,128]{2,1,0:T(8,128)(2,1)}, bf16[4,256,128]{2,1,0:T(8,128)(2,1)}, bf16[4,256,128]{2,1,0:T(8,128)(2,1)}) custom-call(bf16[256,512]{1,0:T(8,128)(2,1)} %get-tuple-element.8.refs_0_, bf16[4,256,128]{2,1,0:T(8,128)(2,1)} %get-tuple-element.9.refs_1_, bf16[4,256,128]{2,1,0:T(8,128)(2,1)} %get-tuple-element.10.refs_2_, ...), custom_call_target="tpu_custom_call" | custom-call | tf_op jit(solution)/shard_map/pallas_call | solution.py:424

commit v6 on v5

--- a/solution.py
+++ b/solution.py
@@ -354,8 +354,16 @@
 
 
 def hand_out(*refs):
-    for source, target in zip(refs[:4], refs[4:]):
-        target[...] = source[...]
+    sources, targets, held, sem = refs[:4], refs[4:8], refs[8:12], refs[12]
+    arrive = [pltpu.make_async_copy(sources[i], held[i], sem.at[i]) for i in range(4)]
+    leave = [pltpu.make_async_copy(held[i], targets[i], sem.at[4 + i]) for i in range(4)]
+    for copy in arrive:
+        copy.start()
+    for i in range(4):
+        arrive[i].wait()
+        leave[i].start()
+    for copy in leave:
+        copy.wait()
 
 
 def per_device(queries, key_vectors, value_vectors, block_perm, out_weight, out_cotangent):
@@ -424,8 +432,10 @@
     return pl.pallas_call(
         hand_out,
         out_shape=shapes,
-        in_specs=[vmem] * 4,
-        out_specs=(vmem,) * 4,
+        in_specs=[in_hbm] * 4,
+        out_specs=(in_hbm,) * 4,
+        scratch_shapes=[pltpu.VMEM(shape.shape, BF) for shape in shapes] + [dma((8,))],
+        compiler_params=pltpu.CompilerParams(vmem_limit_bytes=60 << 20),
     )(*results)
 
 

time: 123 us -> 123 us (level)
  no operation moved by 1% of the time
where the time goes in v6:
time: 123 us
  Pallas kernels  122 us (99%)
    pallas_call x1, Pallas kernels, per_device(): pl.pallas_call(functools.partial(kernel, (heads, tok, width, chips, group...  120 us

profile of v6, /device:TPU:1, one launch (start us, length us, event | category | flops | bytes accessed | tf_op | source)
XLA Modules:
  0.0 122.6 jit_solution(7174496574257066371)
XLA Ops:
  0.6 119.9 %shard_map.93 = (bf16[256,512]{1,0:T(8,128)(2,1)}, bf16[4,256,128]{2,1,0:T(8,128)(2,1)}, bf16[4,256,128]{2,1,0:T(8,128)(2,1)}, bf16[4,256,128]{2,1,0:T(8,128)(2,1)}) custom-call(s32[4,64]{1,0:T(4,128)} %perm_ref.1, bf16[4,256,128]{2,1,0:T(8,128)(2,1)} %q_hbm.1, bf16[32,32,128]{2,1,0:T(8,128)(2,1)} %bitcast.4, bf16[32,32,128]{2,1,0:T(8,128)(2,1)} %bitcast.5, ...), custom_call_target="tpu_custom_call" | custom-call | tf_op jit(solution)/shard_map/pallas_call | solution.py:414
  120.6 2.0 %shard_map.94 = (bf16[256,512]{1,0:T(8,128)(2,1)}, bf16[4,256,128]{2,1,0:T(8,128)(2,1)}, bf16[4,256,128]{2,1,0:T(8,128)(2,1)}, bf16[4,256,128]{2,1,0:T(8,128)(2,1)}) custom-call(bf16[256,512]{1,0:T(8,128)(2,1)} %get-tuple-element.8.refs_0_, bf16[4,256,128]{2,1,0:T(8,128)(2,1)} %get-tuple-element.9.refs_1_, bf16[4,256,128]{2,1,0:T(8,128)(2,1)} %get-tuple-element.10.refs_2_, ...), custom_call_target="tpu_custom_call" | custom-call | tf_op jit(solution)/shard_map/pallas_call | solution.py:432
